TPU v7x, 32 devices: a whole 2x2x4 slice. The times are simulated.
32 devices in a mesh: row: 4 (over z), col: 4 (over y, x), agent: 2 (over core).
Axes of the slice: x: 2, y: 2, z: 4, core: 2. Of those that a mesh axis runs over, the one named last changes fastest.
Arguments:
- raster: bfloat16 [2, 512, 512, 128], P(None, 'row', ('col', 'agent')), may hold values from -6 to 6
- first_kernel: bfloat16 [3, 3, 128, 128], replicated, may hold values from -0.1875 to 0.1875
- first_bias: float32 [128], replicated, may hold values from -3 to 3
- second_kernel: bfloat16 [3, 3, 128, 128], replicated, may hold values from -0.1875 to 0.1875
- second_bias: float32 [128], replicated, may hold values from -3 to 3
- queries: bfloat16 [256, 128], P('agent'), may hold values from -64 to 64
- agent_slot: int32 [256], replicated, may hold values from 0 to 255, each once
- regions: int32 [256, 4], replicated, may hold values from 0 to 8, as said below
Outputs:
- log_heatmap: float32 [2, 512, 512, 256], P(None, 'row', ('col', 'agent'))
Inputs may be any that keep to these rules, and one draw needn't show every extreme that they name: regions[a,0] < regions[a,1] <= 8 and regions[a,2] < regions[a,3] <= 8.
All inputs are finite; a program needn't handle non-finite values.
Results may differ from a plain program's by a relative error of at most 0.0024.
Values may be sent and summed in bfloat16 or wider, within the bound.
A program may use at most 192 MiB of HBM per device.

v0:
```python
import functools

import jax
import jax.numpy as jnp
from jax import lax
from jax.experimental import pallas as pl
from jax.experimental.pallas import tpu as pltpu
from jax.sharding import PartitionSpec as P

BLOCK = 64
PAD = 16
NEG = -1e30
MESH = pl.DeviceIdType.MESH
DIRS = ((-1, 0), (1, 0), (0, -1), (0, 1), (-1, -1), (-1, 1), (1, -1), (1, 1))
BF16 = jnp.bfloat16
F32 = jnp.float32


def field_kernel(
    nr, nc, na, scenes, rows, cols, agents,
    raster, w1, b1, w2, b2, queries, slot, regions,
    l2_out, keys_out, norm_out,
    xp1, xp2, l2, p_edge, p_land, q_edge, q_land, big1, big2, everyone,
    mine, got_q, got_r,
    load_sem, out_sem, h_send, h_recv, k_send, k_recv, sq_send, sq_recv, sr_send, sr_recv,
):
    r = lax.axis_index("row")
    c = lax.axis_index("col")
    a = lax.axis_index("agent")
    nq = nc * na
    q = c * na + a
    pairs = rows // 2
    ch = w1.shape[-1]

    def place(rr, qq):
        return {"row": rr, "col": qq // na, "agent": qq % na}

    def exists(rr, qq):
        return (rr >= 0) & (rr < nr) & (qq >= 0) & (qq < nq)

    barrier = pltpu.get_barrier_semaphore()
    for d in range(1, nr):
        pl.semaphore_signal(barrier, inc=1, device_id=place((r + d) % nr, q), device_id_type=MESH)
    for d in range(1, nq):
        pl.semaphore_signal(barrier, inc=1, device_id=place(r, (q + d) % nq), device_id_type=MESH)
    for dr, dq in DIRS[4:]:
        @pl.when(exists(r + dr, q + dq))
        def _(dr=dr, dq=dq):
            pl.semaphore_signal(barrier, inc=1, device_id=place(r + dr, q + dq), device_id_type=MESH)

    loads = [
        pltpu.make_async_copy(
            raster.at[s], xp1.at[s, pl.ds(2, pairs), :, pl.ds(PAD, cols), :], load_sem.at[s]
        )
        for s in range(scenes)
    ]
    for load in loads:
        load.start()

    for small, big in ((w1, big1), (w2, big2)):
        for i in range(4):
            for j in range(3):
                at = (i * 3 + j) * ch
                big[at : at + ch, 0:ch] = small[i, j] if i < 3 else jnp.zeros((ch, ch), BF16)
                big[at : at + ch, ch : 2 * ch] = small[i - 1, j] if i > 0 else jnp.zeros((ch, ch), BF16)

    def first_refs(s, d):
        dr, dq = DIRS[d]
        dst_k = {-1: pl.ds(pairs + 2, 2), 0: pl.ds(2, pairs), 1: pl.ds(0, 2)}[dr]
        src_k = {-1: pl.ds(0, 2), 0: pl.ds(0, pairs), 1: pl.ds(pairs - 2, 2)}[dr]
        if dq == 0:
            return raster.at[s, src_k], xp1.at[s, dst_k, :, pl.ds(PAD, cols), :]
        side = 1 if dq == 1 else 0
        return p_edge.at[s, side, src_k], p_land.at[s, 1 - side, dst_k]

    def second_refs(s, d):
        dr, dq = DIRS[d]
        dst_r = {-1: pl.ds(rows + 8, 8), 0: pl.ds(8, rows), 1: pl.ds(0, 8)}[dr]
        src_r = {-1: pl.ds(0, 8), 0: pl.ds(0, rows), 1: pl.ds(rows - 8, 8)}[dr]
        if dq == 0:
            src_p = {-1: pl.ds(8, 8), 1: pl.ds(rows, 8)}[dr]
            return xp2.at[s, src_p, pl.ds(PAD, cols), :], xp2.at[s, dst_r, pl.ds(PAD, cols), :]
        side = 1 if dq == 1 else 0
        return q_edge.at[s, side, src_r], q_land.at[s, 1 - side, dst_r]

    def halo(phase, s, d):
        src, dst = (first_refs, second_refs)[phase](s, d)
        dr, dq = DIRS[d]
        return pltpu.make_async_remote_copy(
            src_ref=src, dst_ref=dst,
            send_sem=h_send.at[phase, s, d], recv_sem=h_recv.at[phase, s, d],
            device_id=place(r + dr, q + dq), device_id_type=MESH,
        )

    def start_halo(phase, s):
        for d in (3, 2, 0, 1, 4, 5, 6, 7):
            dr, dq = DIRS[d]

            @pl.when(exists(r + dr, q + dq))
            def _(d=d):
                halo(phase, s, d).start()

    def zero_halo(phase, s):
        for d in range(8):
            dr, dq = DIRS[d]

            @pl.when(jnp.logical_not(exists(r - dr, q - dq)))
            def _(d=d):
                dst = (first_refs, second_refs)[phase](s, d)[1]
                dst[...] = jnp.zeros(dst.shape, BF16)

    def recv_halo(phase, s):
        for d in range(8):
            dr, dq = DIRS[d]

            @pl.when(exists(r - dr, q - dq))
            def _(d=d):
                halo(phase, s, d).wait_recv()

    def sent_halo(phase, s):
        for d in range(8):
            dr, dq = DIRS[d]

            @pl.when(exists(r + dr, q + dq))
            def _(d=d):
                halo(phase, s, d).wait_send()

    for phase in range(2):
        for s in range(scenes):
            zero_halo(phase, s)

    def pack(s):
        @pl.loop(0, pairs // 8)
        def _(t):
            at = pl.ds(2 + t * 8, 8)
            to = pl.ds(t * 8, 8)
            for side, col in ((0, PAD), (1, PAD + cols - 4)):
                for par in range(2):
                    p_edge[s, side, to, 4 * par : 4 * par + 4, :] = xp1[s, at, par, col : col + 4, :]

    loads[0].wait()
    pack(0)
    count = jnp.int32(nr - 1 + nq - 1)
    for dr, dq in DIRS[4:]:
        count = count + exists(r + dr, q + dq).astype(jnp.int32)
    pl.semaphore_wait(barrier, count)
    start_halo(0, 0)

    here = queries.shape[0]

    def key_copy(d):
        other = (a + d) % na
        return pltpu.make_async_remote_copy(
            src_ref=queries, dst_ref=everyone.at[a],
            send_sem=k_send.at[d], recv_sem=k_recv.at[d],
            device_id=place(r, c * na + other), device_id_type=MESH,
        )

    for d in range(1, na):
        key_copy(d).start()
    everyone[a] = queries[...]

    for s in range(1, scenes):
        loads[s].wait()
        pack(s)
        start_halo(0, s)

    for d in range(1, na):
        key_copy(d).wait()
    table = everyone[...].reshape(na * here, ch)
    pick = (lax.broadcasted_iota(jnp.int32, (agents, agents), 0) == slot[...]).astype(F32).astype(BF16)
    keys = lax.dot_general(
        table, pick, (((0,), (0,)), ((), ())), preferred_element_type=F32
    ).astype(BF16)
    keys_out[...] = keys

    bias1 = jnp.concatenate([b1[...], b1[...]], axis=1)
    bias2 = jnp.concatenate([b2[...], b2[...]], axis=1)

    def layer_one(s):
        recv_halo(0, s)
        for k0 in range(0, pairs + 4, 4):
            for par in range(2):
                xp1[s, k0 : k0 + 4, par, PAD - 4 : PAD, :] = p_land[s, 0, k0 : k0 + 4, 4 * par : 4 * par + 4, :]
                xp1[s, k0 : k0 + 4, par, PAD + cols : PAD + cols + 4, :] = (
                    p_land[s, 1, k0 : k0 + 4, 4 * par : 4 * par + 4, :]
                )

        @pl.loop(0, rows // 16)
        def _(g):
            def piece(i, j):
                parts = [
                    xp1[s, pl.ds(8 * g + 4 * h + 2 * i, 2), :, PAD - 4 + 4 * j : PAD - 4 + 4 * j + cols, :]
                    .reshape(4 * cols, ch)
                    for h in range(2)
                ]
                return jnp.concatenate(parts, axis=0)

            lhs = jnp.concatenate([piece(i, j) for i in range(4) for j in range(3)], axis=1)
            out = jnp.dot(lhs, big1[...], preferred_element_type=F32)
            out = jnp.maximum(out + bias1, 0.0).astype(BF16)
            for h in range(2):
                for o in range(2):
                    y = out[h * 4 * cols : (h + 1) * 4 * cols, o * ch : (o + 1) * ch].reshape(4, cols, ch)
                    at = 16 * g + 8 * h + 4 * o
                    xp2[s, pl.ds(8 + at, 4), PAD : PAD + cols, :] = y
                    q_edge[s, 0, pl.ds(at, 4)] = y[:, 0:8]
                    q_edge[s, 1, pl.ds(at, 4)] = y[:, cols - 8 : cols]

        start_halo(1, s)

    def layer_two(s):
        recv_halo(1, s)
        for k0 in range(0, rows + 16, 16):
            xp2[s, k0 : k0 + 16, PAD - 8 : PAD, :] = q_land[s, 0, k0 : k0 + 16]
            xp2[s, k0 : k0 + 16, PAD + cols : PAD + cols + 8, :] = q_land[s, 1, k0 : k0 + 16]

        peak = jnp.full((1, agents), NEG, F32)
        mass = jnp.zeros((1, agents), F32)
        for block in range(rows // BLOCK):
            def step(t, carry):
                top, total = carry
                g = block * (BLOCK // 16) + t

                def piece(i, j):
                    return xp2[
                        s, pl.ds(16 * g + 8 * i, 8), PAD - 8 + 8 * j : PAD - 8 + 8 * j + cols, :
                    ].reshape(8 * cols, ch)

                lhs = jnp.concatenate([piece(i, j) for i in range(4) for j in range(3)], axis=1)
                out = jnp.dot(lhs, big2[...], preferred_element_type=F32)
                out = jnp.maximum(out + bias2, 0.0).astype(BF16)
                for o in range(2):
                    y = out[:, o * ch : (o + 1) * ch]
                    l2[s, pl.ds(16 * g + 8 * o, 8)] = y.reshape(8, cols, ch)
                    z = jnp.dot(y, keys_out[...], preferred_element_type=F32).reshape(cols, 8, agents)
                    new = jnp.maximum(top, jnp.max(z, axis=0))
                    total = total * jnp.exp(top - new) + jnp.sum(jnp.exp(z - new[None]), axis=0)
                    top = new
                return top, total

            top, total = lax.fori_loop(
                0, BLOCK // 16, step,
                (jnp.full((8, agents), NEG, F32), jnp.zeros((8, agents), F32)),
            )
            high = jnp.max(top, axis=0, keepdims=True)
            part = jnp.sum(total * jnp.exp(top - high), axis=0, keepdims=True)
            block_row = r * (rows // BLOCK) + block
            block_col = q * cols // BLOCK
            ok = (
                (regions[0:1] <= block_row) & (block_row < regions[1:2])
                & (regions[2:3] <= block_col) & (block_col < regions[3:4])
            )
            high = jnp.where(ok, high, NEG)
            part = jnp.where(ok, part, 0.0)
            new = jnp.maximum(peak, high)
            mass = mass * jnp.exp(peak - new) + part * jnp.exp(high - new)
            peak = new
        return peak, mass

    for s in range(scenes):
        layer_one(s)
    peaks, masses = [], []
    outs = []
    for s in range(scenes):
        peak, mass = layer_two(s)
        peaks.append(peak)
        masses.append(mass)
        out = pltpu.make_async_copy(l2.at[s], l2_out.at[s], out_sem.at[s])
        out.start()
        outs.append(out)

    def stat_copy(src, got, send, recv, me, rr, qq, d):
        return pltpu.make_async_remote_copy(
            src_ref=src, dst_ref=got.at[d], send_sem=send.at[d], recv_sem=recv.at[d],
            device_id=place(rr, qq), device_id_type=MESH,
        )

    def merge(tops, parts):
        top = functools.reduce(jnp.maximum, tops)
        return top, functools.reduce(jnp.add, [p * jnp.exp(t - top) for t, p in zip(tops, parts)])

    top = jnp.concatenate(peaks, axis=0)
    part = jnp.concatenate(masses, axis=0)
    for stage, (size, got, send, recv) in enumerate(
        ((nq, got_q, sq_send, sq_recv), (nr, got_r, sr_send, sr_recv))
    ):
        mine[stage, 0] = top
        mine[stage, 1] = part
        copies = []
        for d in range(1, size):
            rr, qq = (r, (q + d) % nq) if stage == 0 else ((r + d) % nr, q)
            copies.append(stat_copy(mine.at[stage], got, send, recv, None, rr, qq, d))
            copies[-1].start()
        for copy in copies:
            copy.wait()
        top, part = merge(
            [top] + [got[d, 0] for d in range(1, size)],
            [part] + [got[d, 1] for d in range(1, size)],
        )
    norm_out[...] = top + jnp.log(part)

    for phase in range(2):
        for s in range(scenes):
            sent_halo(phase, s)
    for out in outs:
        out.wait()


def heat_kernel(field, keys, norm, out):
    out[0] = jnp.dot(field[0], keys[...], preferred_element_type=F32) - norm[0]


def shards(nr, nc, na, raster, w1, b1, w2, b2, queries, slot, regions):
    scenes, rows, cols, ch = raster.shape
    agents = slot.shape[0]
    nq = nc * na
    vmem = pl.BlockSpec(memory_space=pltpu.VMEM)
    anywhere = pl.BlockSpec(memory_space=pl.ANY)
    dma = pltpu.SemaphoreType.DMA
    field, keys, norm = pl.pallas_call(
        functools.partial(field_kernel, nr, nc, na, scenes, rows, cols, agents),
        out_shape=(
            jax.ShapeDtypeStruct((scenes, rows, cols, ch), BF16),
            jax.ShapeDtypeStruct((ch, agents), BF16),
            jax.ShapeDtypeStruct((scenes, agents), F32),
        ),
        in_specs=[anywhere] + [vmem] * 7,
        out_specs=(anywhere, vmem, vmem),
        scratch_shapes=[
            pltpu.VMEM((scenes, rows // 2 + 4, 2, cols + 2 * PAD, ch), BF16),
            pltpu.VMEM((scenes, rows + 16, cols + 2 * PAD, ch), BF16),
            pltpu.VMEM((scenes, rows, cols, ch), BF16),
            pltpu.VMEM((scenes, 2, rows // 2, 8, ch), BF16),
            pltpu.VMEM((scenes, 2, rows // 2 + 4, 8, ch), BF16),
            pltpu.VMEM((scenes, 2, rows, 8, ch), BF16),
            pltpu.VMEM((scenes, 2, rows + 16, 8, ch), BF16),
            pltpu.VMEM((12 * ch, 2 * ch), BF16),
            pltpu.VMEM((12 * ch, 2 * ch), BF16),
            pltpu.VMEM((na,) + queries.shape, BF16),
            pltpu.VMEM((2, 2, scenes, agents), F32),
            pltpu.VMEM((nq, 2, scenes, agents), F32),
            pltpu.VMEM((nr, 2, scenes, agents), F32),
            dma((scenes,)),
            dma((scenes,)),
            dma((2, scenes, 8)),
            dma((2, scenes, 8)),
            dma((na,)),
            dma((na,)),
            dma((nq,)),
            dma((nq,)),
            dma((nr,)),
            dma((nr,)),
        ],
        compiler_params=pltpu.CompilerParams(
            collective_id=0, has_side_effects=True, vmem_limit_bytes=60 * 1024 * 1024
        ),
        name="field",
    )(
        raster.reshape(scenes, rows // 2, 2, cols, ch), w1, b1.reshape(1, -1), w2, b2.reshape(1, -1),
        queries, slot.reshape(1, -1), regions.T,
    )
    cells = rows * cols
    step = min(2048, cells)
    heat = pl.pallas_call(
        heat_kernel,
        grid=(scenes, cells // step),
        out_shape=jax.ShapeDtypeStruct((scenes, cells, agents), F32),
        in_specs=[
            pl.BlockSpec((1, step, ch), lambda s, t: (s, t, 0)),
            pl.BlockSpec((ch, agents), lambda s, t: (0, 0)),
            pl.BlockSpec((1, 1, agents), lambda s, t: (s, 0, 0)),
        ],
        out_specs=pl.BlockSpec((1, step, agents), lambda s, t: (s, t, 0)),
        name="heat",
    )(field.reshape(scenes, cells, ch), keys, norm.reshape(scenes, 1, agents))
    return heat.reshape(scenes, rows, cols, agents)


def solution(mesh):
    in_specs = (P(None, "row", ("col", "agent"), None), P(), P(), P(), P(), P("agent", None), P(), P())
    out_specs = P(None, "row", ("col", "agent"), None)
    sizes = (mesh.shape["row"], mesh.shape["col"], mesh.shape["agent"])
    return jax.shard_map(
        functools.partial(shards, *sizes), mesh=mesh, in_specs=in_specs, out_specs=out_specs, check_vma=False
    )
```

profile of v0, /device:TPU:0, one launch (start us, length us, event | category | flops | bytes accessed | tf_op | source)
XLA Modules:
  0.0 61.6 jit_solution(3598341696095334043)
XLA Ops:
  0.0 50.5 %field.1 = (bf16[2,128,64,128]{3,2,1,0:T(8,128)(2,1)}, bf16[128,256]{1,0:T(8,128)(2,1)}, f32[2,256]{1,0:T(2,128)}) custom-call(bf16[2,64,2,64,128]{4,3,2,1,0:T(8,128)(2,1)} %bitcast.7, bf16[3,3,128,128]{3,2,1,0:T(8,128)(2,1)} %w1.1, f32[1,128]{1,0:T(1,128)} %bitcast.11, bf16[3,3,128,128]{3,2,1,0:T(8,128)(2,1)} %w2.1, f32[1,128]{1,0:T(1,128)} %bitcast.12, ...), custom_call_target="tpu_custom_call" | custom-call | tf_op jit(solution)/shard_map/field/pallas_call | solution.py:321
  50.5 1.2 %reshape.26.norm = f32[2,1,256]{2,1,0:T(1,128)} reshape(f32[2,256]{1,0:T(2,128)} %get-tuple-element.10) | data formatting | bytes 4096 | tf_op jit(solution)/shard_map/reshape | solution.py:376
  51.8 9.8 %heat.1 = f32[2,8192,256]{2,1,0:T(8,128)} custom-call(bf16[2,8192,128]{2,1,0:T(8,128)(2,1)} %bitcast.8, bf16[128,256]{1,0:T(8,128)(2,1)} %get-tuple-element.9.keys, f32[2,1,256]{2,1,0:T(1,128)} %reshape.26.norm), custom_call_target="tpu_custom_call" | custom-call | tf_op jit(solution)/shard_map/heat/pallas_call | solution.py:365
where the time goes:
time: 62 us; the launch traced here: 61.6 us
  Pallas kernels  60.4 us (97%)
  local copies, waits for them, and re-layouts  1.25 us (2%)
    pallas_call x1, Pallas kernels, shards(): pl.pallas_call(functools.partial(field_kernel, nr, nc, na, scenes, rows,...  50.5 us
    pallas_call x1, Pallas kernels, shards(): pl.pallas_call(heat_kernel, grid=(scenes, cells // step), out_shape=jax.S...  9.84 us
    reshape x1, local copies, waits for them, and re-layouts, shards(): norm.reshape(scenes, 1, agents)  1.25 us

commit v1 on v0

--- a/solution.py
+++ b/solution.py
@@ -20,7 +20,7 @@
     nr, nc, na, scenes, rows, cols, agents,
     raster, w1, b1, w2, b2, queries, slot, regions,
     l2_out, keys_out, norm_out,
-    xp1, xp2, l2, p_edge, p_land, q_edge, q_land, big1, big2, everyone,
+    xp1, xp2, l2, z_ref, tops, sums, p_edge, p_land, q_edge, q_land, big1, big2, everyone,
     mine, got_q, got_r,
     load_sem, out_sem, h_send, h_recv, k_send, k_recv, sq_send, sq_recv, sr_send, sr_recv,
 ):
@@ -215,34 +215,29 @@
             xp2[s, k0 : k0 + 16, PAD - 8 : PAD, :] = q_land[s, 0, k0 : k0 + 16]
             xp2[s, k0 : k0 + 16, PAD + cols : PAD + cols + 8, :] = q_land[s, 1, k0 : k0 + 16]
 
+        @pl.loop(0, steps)
+        def _(t):
+            fold(s * steps + t - 2)
+            score(s * steps + t - 1)
+
+            def piece(i, j):
+                return xp2[
+                    s, pl.ds(16 * t + 8 * i, 8), PAD - 8 + 8 * j : PAD - 8 + 8 * j + cols, :
+                ].reshape(8 * cols, ch)
+
+            lhs = jnp.concatenate([piece(i, j) for i in range(4) for j in range(3)], axis=1)
+            out = jnp.dot(lhs, big2[...], preferred_element_type=F32)
+            out = jnp.maximum(out + bias2, 0.0).astype(BF16)
+            for o in range(2):
+                at = s * rows + 16 * t + 8 * o
+                l2[pl.ds(at, 8)] = out[:, o * ch : (o + 1) * ch].reshape(8, cols, ch)
+
+    def settle(s):
         peak = jnp.full((1, agents), NEG, F32)
         mass = jnp.zeros((1, agents), F32)
         for block in range(rows // BLOCK):
-            def step(t, carry):
-                top, total = carry
-                g = block * (BLOCK // 16) + t
-
-                def piece(i, j):
-                    return xp2[
-                        s, pl.ds(16 * g + 8 * i, 8), PAD - 8 + 8 * j : PAD - 8 + 8 * j + cols, :
-                    ].reshape(8 * cols, ch)
-
-                lhs = jnp.concatenate([piece(i, j) for i in range(4) for j in range(3)], axis=1)
-                out = jnp.dot(lhs, big2[...], preferred_element_type=F32)
-                out = jnp.maximum(out + bias2, 0.0).astype(BF16)
-                for o in range(2):
-                    y = out[:, o * ch : (o + 1) * ch]
-                    l2[s, pl.ds(16 * g + 8 * o, 8)] = y.reshape(8, cols, ch)
-                    z = jnp.dot(y, keys_out[...], preferred_element_type=F32).reshape(cols, 8, agents)
-                    new = jnp.maximum(top, jnp.max(z, axis=0))
-                    total = total * jnp.exp(top - new) + jnp.sum(jnp.exp(z - new[None]), axis=0)
-                    top = new
-                return top, total
-
-            top, total = lax.fori_loop(
-                0, BLOCK // 16, step,
-                (jnp.full((8, agents), NEG, F32), jnp.zeros((8, agents), F32)),
-            )
+            top = tops[s * (rows // BLOCK) + block]
+            total = sums[s * (rows // BLOCK) + block]
             high = jnp.max(top, axis=0, keepdims=True)
             part = jnp.sum(total * jnp.exp(top - high), axis=0, keepdims=True)
             block_row = r * (rows // BLOCK) + block
@@ -258,17 +253,56 @@
             peak = new
         return peak, mass
 
+    steps = rows // 16
+    spare = scenes * rows // BLOCK
+
+    def score(u):
+        at = 16 * jnp.maximum(u, 0) if not isinstance(u, int) else 16 * u
+        y = l2[pl.ds(at, 16)].reshape(16 * cols, ch)
+        z_ref[...] = jnp.dot(y, keys_out[...], preferred_element_type=F32)
+
+    def fold(u):
+        slot = u // (BLOCK // 16) if isinstance(u, int) else jnp.where(u >= 0, u // (BLOCK // 16), spare)
+        top, total = tops[slot], sums[slot]
+        size = 64
+        chunks = 16 * cols // size
+        maxes = [top]
+        for k in range(chunks):
+            m = jnp.max(z_ref[k * size : (k + 1) * size].reshape(size // 8, 8, agents), axis=0)
+            if k < 4:
+                maxes.append(m)
+            else:
+                maxes[1 + k % 4] = jnp.maximum(maxes[1 + k % 4], m)
+        new = functools.reduce(jnp.maximum, maxes)
+        total = total * jnp.exp(top - new)
+        for k in range(chunks):
+            z = z_ref[k * size : (k + 1) * size].reshape(size // 8, 8, agents)
+            total = total + jnp.sum(jnp.exp(z - new[None]), axis=0)
+        tops[slot] = new
+        sums[slot] = total
+
+    z_ref[...] = jnp.zeros(z_ref.shape, F32)
+    l2[0:16] = jnp.zeros((16, cols, ch), BF16)
+    tops[...] = jnp.full(tops.shape, NEG, F32)
+    sums[...] = jnp.zeros(sums.shape, F32)
+
     for s in range(scenes):
         layer_one(s)
     peaks, masses = [], []
     outs = []
     for s in range(scenes):
-        peak, mass = layer_two(s)
+        layer_two(s)
+        if s == scenes - 1:
+            fold(scenes * steps - 2)
+            score(scenes * steps - 1)
+            fold(scenes * steps - 1)
+        out = pltpu.make_async_copy(l2.at[pl.ds(s * rows, rows)], l2_out.at[s], out_sem.at[s])
+        out.start()
+        outs.append(out)
+    for s in range(scenes):
+        peak, mass = settle(s)
         peaks.append(peak)
         masses.append(mass)
-        out = pltpu.make_async_copy(l2.at[s], l2_out.at[s], out_sem.at[s])
-        out.start()
-        outs.append(out)
 
     def stat_copy(src, got, send, recv, me, rr, qq, d):
         return pltpu.make_async_remote_copy(
@@ -307,8 +341,32 @@
         out.wait()
 
 
-def heat_kernel(field, keys, norm, out):
-    out[0] = jnp.dot(field[0], keys[...], preferred_element_type=F32) - norm[0]
+def heat_kernel(field, keys, norm, out, cells, heat, in_sem, out_sem):
+    scenes, total, _ = field.shape
+    parts, size = cells.shape[0], cells.shape[1]
+    slots = heat.shape[0]
+    per = total // size
+    loads = []
+    for t in range(parts):
+        load = pltpu.make_async_copy(
+            field.at[t // per, pl.ds(t % per * size, size)], cells.at[t], in_sem.at[t]
+        )
+        load.start()
+        loads.append(load)
+    stores = []
+    for t in range(parts):
+        if t >= slots:
+            stores[t - slots].wait()
+        loads[t].wait()
+        s = t // per
+        heat[t % slots] = jnp.dot(cells[t], keys[...], preferred_element_type=F32) - norm[s : s + 1]
+        store = pltpu.make_async_copy(
+            heat.at[t % slots], out.at[s, pl.ds(t % per * size, size)], out_sem.at[t % slots]
+        )
+        store.start()
+        stores.append(store)
+    for store in stores[max(parts - slots, 0):]:
+        store.wait()
 
 
 def shards(nr, nc, na, raster, w1, b1, w2, b2, queries, slot, regions):
@@ -330,7 +388,10 @@
         scratch_shapes=[
             pltpu.VMEM((scenes, rows // 2 + 4, 2, cols + 2 * PAD, ch), BF16),
             pltpu.VMEM((scenes, rows + 16, cols + 2 * PAD, ch), BF16),
-            pltpu.VMEM((scenes, rows, cols, ch), BF16),
+            pltpu.VMEM((scenes * rows, cols, ch), BF16),
+            pltpu.VMEM((16 * cols, agents), F32),
+            pltpu.VMEM((scenes * rows // BLOCK + 1, 8, agents), F32),
+            pltpu.VMEM((scenes * rows // BLOCK + 1, 8, agents), F32),
             pltpu.VMEM((scenes, 2, rows // 2, 8, ch), BF16),
             pltpu.VMEM((scenes, 2, rows // 2 + 4, 8, ch), BF16),
             pltpu.VMEM((scenes, 2, rows, 8, ch), BF16),
@@ -361,19 +422,22 @@
         queries, slot.reshape(1, -1), regions.T,
     )
     cells = rows * cols
-    step = min(2048, cells)
+    size = min(2048, cells)
+    parts = scenes * cells // size
+    slots = min(4, parts)
     heat = pl.pallas_call(
         heat_kernel,
-        grid=(scenes, cells // step),
         out_shape=jax.ShapeDtypeStruct((scenes, cells, agents), F32),
-        in_specs=[
-            pl.BlockSpec((1, step, ch), lambda s, t: (s, t, 0)),
-            pl.BlockSpec((ch, agents), lambda s, t: (0, 0)),
-            pl.BlockSpec((1, 1, agents), lambda s, t: (s, 0, 0)),
+        in_specs=[anywhere, vmem, vmem],
+        out_specs=anywhere,
+        scratch_shapes=[
+            pltpu.VMEM((parts, size, ch), BF16),
+            pltpu.VMEM((slots, size, agents), F32),
+            dma((parts,)),
+            dma((slots,)),
         ],
-        out_specs=pl.BlockSpec((1, step, agents), lambda s, t: (s, t, 0)),
         name="heat",
-    )(field.reshape(scenes, cells, ch), keys, norm.reshape(scenes, 1, agents))
+    )(field.reshape(scenes, cells, ch), keys, norm)
     return heat.reshape(scenes, rows, cols, agents)
 
 

time: 62 us -> 55.2 us (0.89)
  Pallas kernels: 60.4 us -> 55 us
  local copies, waits for them, and re-layouts: 1.25 us -> 0 us
    pallas_call x1, Pallas kernels: 50.5 us -> 46.3 us  [shards(): pl.pallas_call(functools.partial(field_kernel, nr, nc, na, scenes, rows,...]
    reshape x1 -> x0, local copies, waits for them, and re-layouts: 1.25 us -> none  [shards(): norm.reshape(scenes, 1, agents)]
    pallas_call x1, Pallas kernels: 9.84 us -> 8.74 us  [shards(): pl.pallas_call(heat_kernel, out_shape=jax.ShapeDtypeStruct((scenes, cells...]
where the time goes in v1:
time: 55.2 us; the launch traced here: 55 us
  Pallas kernels  55 us (100%)
    pallas_call x1, Pallas kernels, shards(): pl.pallas_call(functools.partial(field_kernel, nr, nc, na, scenes, rows,...  46.3 us
    pallas_call x1, Pallas kernels, shards(): pl.pallas_call(heat_kernel, out_shape=jax.ShapeDtypeStruct((scenes, cells...  8.74 us

profile of v1, /device:TPU:0, one launch (start us, length us, event | category | flops | bytes accessed | tf_op | source)
XLA Modules:
  0.0 55.0 jit_solution(6602301960656093798)
XLA Ops:
  0.0 46.3 %field.1 = (bf16[2,128,64,128]{3,2,1,0:T(8,128)(2,1)}, bf16[128,256]{1,0:T(8,128)(2,1)}, f32[2,256]{1,0:T(2,128)}) custom-call(bf16[2,64,2,64,128]{4,3,2,1,0:T(8,128)(2,1)} %bitcast.7, bf16[3,3,128,128]{3,2,1,0:T(8,128)(2,1)} %w1.1, f32[1,128]{1,0:T(1,128)} %bitcast.11, bf16[3,3,128,128]{3,2,1,0:T(8,128)(2,1)} %w2.1, f32[1,128]{1,0:T(1,128)} %bitcast.12, ...), custom_call_target="tpu_custom_call" | custom-call | tf_op jit(solution)/shard_map/field/pallas_call | solution.py:379
  46.3 8.7 %heat.1 = f32[2,8192,256]{2,1,0:T(8,128)} custom-call(bf16[2,8192,128]{2,1,0:T(8,128)(2,1)} %bitcast.8, bf16[128,256]{1,0:T(8,128)(2,1)} %get-tuple-element.9.keys, f32[2,256]{1,0:T(2,128)} %get-tuple-element.10.norm), custom_call_target="tpu_custom_call" | custom-call | tf_op jit(solution)/shard_map/heat/pallas_call | solution.py:428

commit v2 on v1

--- a/solution.py
+++ b/solution.py
@@ -12,6 +12,8 @@
 NEG = -1e30
 MESH = pl.DeviceIdType.MESH
 DIRS = ((-1, 0), (1, 0), (0, -1), (0, 1), (-1, -1), (-1, 1), (1, -1), (1, 1))
+FIRST = (3, 2, 0, 1, 4, 5, 6, 7, 9, 8)
+PIECES = DIRS + ((0, -1), (0, 1))
 BF16 = jnp.bfloat16
 F32 = jnp.float32
 
@@ -31,6 +33,7 @@
     q = c * na + a
     pairs = rows // 2
     ch = w1.shape[-1]
+    cut1 = pairs // 2 + 2
 
     def place(rr, qq):
         return {"row": rr, "col": qq // na, "agent": qq % na}
@@ -65,18 +68,20 @@
                 big[at : at + ch, ch : 2 * ch] = small[i - 1, j] if i > 0 else jnp.zeros((ch, ch), BF16)
 
     def first_refs(s, d):
-        dr, dq = DIRS[d]
-        dst_k = {-1: pl.ds(pairs + 2, 2), 0: pl.ds(2, pairs), 1: pl.ds(0, 2)}[dr]
-        src_k = {-1: pl.ds(0, 2), 0: pl.ds(0, pairs), 1: pl.ds(pairs - 2, 2)}[dr]
+        dr, dq = PIECES[d]
+        low, high = (cut1, pairs) if d >= 8 else (0, cut1)
+        dst_k = {-1: pl.ds(pairs + 2, 2), 0: pl.ds(2 + low, high - low), 1: pl.ds(0, 2)}[dr]
+        src_k = {-1: pl.ds(0, 2), 0: pl.ds(low, high - low), 1: pl.ds(pairs - 2, 2)}[dr]
         if dq == 0:
             return raster.at[s, src_k], xp1.at[s, dst_k, :, pl.ds(PAD, cols), :]
         side = 1 if dq == 1 else 0
         return p_edge.at[s, side, src_k], p_land.at[s, 1 - side, dst_k]
 
     def second_refs(s, d):
-        dr, dq = DIRS[d]
-        dst_r = {-1: pl.ds(rows + 8, 8), 0: pl.ds(8, rows), 1: pl.ds(0, 8)}[dr]
-        src_r = {-1: pl.ds(0, 8), 0: pl.ds(0, rows), 1: pl.ds(rows - 8, 8)}[dr]
+        dr, dq = PIECES[d]
+        low, high = (rows // 2, rows) if d >= 8 else (0, rows // 2)
+        dst_r = {-1: pl.ds(rows + 8, 8), 0: pl.ds(8 + low, high - low), 1: pl.ds(0, 8)}[dr]
+        src_r = {-1: pl.ds(0, 8), 0: pl.ds(low, high - low), 1: pl.ds(rows - 8, 8)}[dr]
         if dq == 0:
             src_p = {-1: pl.ds(8, 8), 1: pl.ds(rows, 8)}[dr]
             return xp2.at[s, src_p, pl.ds(PAD, cols), :], xp2.at[s, dst_r, pl.ds(PAD, cols), :]
@@ -85,41 +90,41 @@
 
     def halo(phase, s, d):
         src, dst = (first_refs, second_refs)[phase](s, d)
-        dr, dq = DIRS[d]
+        dr, dq = PIECES[d]
         return pltpu.make_async_remote_copy(
             src_ref=src, dst_ref=dst,
             send_sem=h_send.at[phase, s, d], recv_sem=h_recv.at[phase, s, d],
             device_id=place(r + dr, q + dq), device_id_type=MESH,
         )
 
-    def start_halo(phase, s):
-        for d in (3, 2, 0, 1, 4, 5, 6, 7):
-            dr, dq = DIRS[d]
+    def start_halo(phase, s, picked):
+        for d in picked:
+            dr, dq = PIECES[d]
 
             @pl.when(exists(r + dr, q + dq))
             def _(d=d):
                 halo(phase, s, d).start()
 
     def zero_halo(phase, s):
-        for d in range(8):
-            dr, dq = DIRS[d]
+        for d in range(10):
+            dr, dq = PIECES[d]
 
             @pl.when(jnp.logical_not(exists(r - dr, q - dq)))
             def _(d=d):
                 dst = (first_refs, second_refs)[phase](s, d)[1]
                 dst[...] = jnp.zeros(dst.shape, BF16)
 
-    def recv_halo(phase, s):
-        for d in range(8):
-            dr, dq = DIRS[d]
+    def recv_halo(phase, s, picked):
+        for d in picked:
+            dr, dq = PIECES[d]
 
             @pl.when(exists(r - dr, q - dq))
             def _(d=d):
                 halo(phase, s, d).wait_recv()
 
     def sent_halo(phase, s):
-        for d in range(8):
-            dr, dq = DIRS[d]
+        for d in range(10):
+            dr, dq = PIECES[d]
 
             @pl.when(exists(r + dr, q + dq))
             def _(d=d):
@@ -144,7 +149,7 @@
     for dr, dq in DIRS[4:]:
         count = count + exists(r + dr, q + dq).astype(jnp.int32)
     pl.semaphore_wait(barrier, count)
-    start_halo(0, 0)
+    start_halo(0, 0, FIRST)
 
     here = queries.shape[0]
 
@@ -163,7 +168,7 @@
     for s in range(1, scenes):
         loads[s].wait()
         pack(s)
-        start_halo(0, s)
+        start_halo(0, s, FIRST)
 
     for d in range(1, na):
         key_copy(d).wait()
@@ -178,39 +183,48 @@
     bias2 = jnp.concatenate([b2[...], b2[...]], axis=1)
 
     def layer_one(s):
-        recv_halo(0, s)
-        for k0 in range(0, pairs + 4, 4):
-            for par in range(2):
-                xp1[s, k0 : k0 + 4, par, PAD - 4 : PAD, :] = p_land[s, 0, k0 : k0 + 4, 4 * par : 4 * par + 4, :]
-                xp1[s, k0 : k0 + 4, par, PAD + cols : PAD + cols + 4, :] = (
-                    p_land[s, 1, k0 : k0 + 4, 4 * par : 4 * par + 4, :]
-                )
-
-        @pl.loop(0, rows // 16)
-        def _(g):
+        def unpack(low, high):
+            for k0 in range(low, high, 4):
+                for par in range(2):
+                    for side, col in ((0, PAD - 4), (1, PAD + cols)):
+                        xp1[s, k0 : k0 + 4, par, col : col + 4, :] = (
+                            p_land[s, side, k0 : k0 + 4, 4 * par : 4 * par + 4, :]
+                        )
+
+        def sweep(low, high):
+            pl.loop(low // 32, high // 32)(body)
+
+        def body(g):
             def piece(i, j):
                 parts = [
-                    xp1[s, pl.ds(8 * g + 4 * h + 2 * i, 2), :, PAD - 4 + 4 * j : PAD - 4 + 4 * j + cols, :]
+                    xp1[s, pl.ds(16 * g + 4 * h + 2 * i, 2), :, PAD - 4 + 4 * j : PAD - 4 + 4 * j + cols, :]
                     .reshape(4 * cols, ch)
-                    for h in range(2)
+                    for h in range(4)
                 ]
                 return jnp.concatenate(parts, axis=0)
 
             lhs = jnp.concatenate([piece(i, j) for i in range(4) for j in range(3)], axis=1)
             out = jnp.dot(lhs, big1[...], preferred_element_type=F32)
             out = jnp.maximum(out + bias1, 0.0).astype(BF16)
-            for h in range(2):
+            for h in range(4):
                 for o in range(2):
                     y = out[h * 4 * cols : (h + 1) * 4 * cols, o * ch : (o + 1) * ch].reshape(4, cols, ch)
-                    at = 16 * g + 8 * h + 4 * o
+                    at = 32 * g + 8 * h + 4 * o
                     xp2[s, pl.ds(8 + at, 4), PAD : PAD + cols, :] = y
                     q_edge[s, 0, pl.ds(at, 4)] = y[:, 0:8]
                     q_edge[s, 1, pl.ds(at, 4)] = y[:, cols - 8 : cols]
 
-        start_halo(1, s)
+        recv_halo(0, s, range(8))
+        unpack(0, cut1 + 2)
+        sweep(0, rows // 2)
+        start_halo(1, s, (3, 2, 0, 4, 5))
+        recv_halo(0, s, (8, 9))
+        unpack(cut1 + 2, pairs + 4)
+        sweep(rows // 2, rows)
+        start_halo(1, s, (9, 8, 1, 6, 7))
 
     def layer_two(s):
-        recv_halo(1, s)
+        recv_halo(1, s, range(10))
         for k0 in range(0, rows + 16, 16):
             xp2[s, k0 : k0 + 16, PAD - 8 : PAD, :] = q_land[s, 0, k0 : k0 + 16]
             xp2[s, k0 : k0 + 16, PAD + cols : PAD + cols + 8, :] = q_land[s, 1, k0 : k0 + 16]
@@ -404,8 +418,8 @@
             pltpu.VMEM((nr, 2, scenes, agents), F32),
             dma((scenes,)),
             dma((scenes,)),
-            dma((2, scenes, 8)),
-            dma((2, scenes, 8)),
+            dma((2, scenes, 10)),
+            dma((2, scenes, 10)),
             dma((na,)),
             dma((na,)),
             dma((nq,)),

time: 55.2 us -> 52 us (0.942)
  Pallas kernels: 55 us -> 51.9 us
    pallas_call x1, Pallas kernels: 46.3 us -> 43.1 us  [shards(): pl.pallas_call(functools.partial(field_kernel, nr, nc, na, scenes, rows,...]
where the time goes in v2:
time: 52 us; the launch traced here: 51.9 us
  Pallas kernels  51.9 us (100%)
    pallas_call x1, Pallas kernels, shards(): pl.pallas_call(functools.partial(field_kernel, nr, nc, na, scenes, rows,...  43.1 us
    pallas_call x1, Pallas kernels, shards(): pl.pallas_call(heat_kernel, out_shape=jax.ShapeDtypeStruct((scenes, cells...  8.74 us

profile of v2, /device:TPU:0, one launch (start us, length us, event | category | flops | bytes accessed | tf_op | source)
XLA Modules:
  0.0 51.9 jit_solution(3962678054271914637)
XLA Ops:
  0.0 43.1 %field.1 = (bf16[2,128,64,128]{3,2,1,0:T(8,128)(2,1)}, bf16[128,256]{1,0:T(8,128)(2,1)}, f32[2,256]{1,0:T(2,128)}) custom-call(bf16[2,64,2,64,128]{4,3,2,1,0:T(8,128)(2,1)} %bitcast.7, bf16[3,3,128,128]{3,2,1,0:T(8,128)(2,1)} %w1.1, f32[1,128]{1,0:T(1,128)} %bitcast.11, bf16[3,3,128,128]{3,2,1,0:T(8,128)(2,1)} %w2.1, f32[1,128]{1,0:T(1,128)} %bitcast.12, ...), custom_call_target="tpu_custom_call" | custom-call | tf_op jit(solution)/shard_map/field/pallas_call | solution.py:393
  43.1 8.7 %heat.1 = f32[2,8192,256]{2,1,0:T(8,128)} custom-call(bf16[2,8192,128]{2,1,0:T(8,128)(2,1)} %bitcast.8, bf16[128,256]{1,0:T(8,128)(2,1)} %get-tuple-element.9.keys, f32[2,256]{1,0:T(2,128)} %get-tuple-element.10.norm), custom_call_target="tpu_custom_call" | custom-call | tf_op jit(solution)/shard_map/heat/pallas_call | solution.py:442
